TPU v7x, 32 devices: a whole 2x2x4 slice. The times are simulated.
32 devices in a mesh: dp: 4 (over x, core), expert: 8 (over z, y).
Axes of the slice: x: 2, y: 2, z: 4, core: 2. Of those that a mesh axis runs over, the one named last changes fastest.
Arguments:
- tokens: bfloat16 [4096, 4096], P(('dp', 'expert')), may hold values from -6 to 6
- router: bfloat16 [4096, 8], replicated, may hold values from -0.09375 to 0.09375
- price: float32 [8], replicated, may hold values from -1 to 1
- w_in: bfloat16 [8, 4096, 8192], P('expert', None, 'dp'), may hold values from -0.09375 to 0.09375
- w_out: bfloat16 [8, 8192, 4096], P('expert', 'dp'), may hold values from -0.0625 to 0.0625
- assign: int32 [4096], P(('dp', 'expert')), may hold values from 0 to 7, as said below
Outputs:
- mixed: bfloat16 [4096, 4096], P(('dp', 'expert'))
- new_price: float32 [8], replicated
Inputs may be any that keep to these rules, and one draw needn't show every extreme that they name: `assign`: every expert is named by exactly 512 tokens in all, and by at most 24 of the 128 tokens of one device (aligned blocks of 128 rows); on every device some expert is named exactly 24 times, and the experts' loads on one device are, in some order, the same 8 numbers on every device.
All inputs are finite; a program needn't handle non-finite values.
Results may differ from a plain program's by a relative error of at most 0.013.
Values may be sent and summed in bfloat16 or wider, within the bound.
A program may use at most 128 MiB of HBM per device.

v0:
```python
import jax
import jax.numpy as jnp
from jax import lax
from jax.sharding import PartitionSpec as P

BID_STEP = 0.01


def shards(tokens, router, price, w_in, w_out, assign):
    experts = router.shape[1]
    width = tokens.shape[1]
    local_tokens = tokens.shape[0]
    capacity = 3 * local_tokens // (2 * experts)
    first = w_in[0]
    second = w_out[0]
    affinity = jnp.dot(tokens, router, preferred_element_type=jnp.float32)
    onehot = assign[:, None] == jnp.arange(experts, dtype=jnp.int32)[None, :]
    own = jnp.sum(jnp.where(onehot, affinity, 0.0), axis=1)
    rival = jnp.max(jnp.where(onehot, -1e30, affinity - price[None, :]), axis=1)
    bid = own - rival + BID_STEP
    local_best = jnp.max(jnp.where(onehot, bid[:, None], -1e30), axis=0)
    new_price = lax.pmax(local_best, ("dp", "expert"))
    lower = (jnp.arange(local_tokens)[:, None] >= jnp.arange(local_tokens)[None, :]).astype(
        jnp.bfloat16
    )
    running = jnp.dot(lower, onehot.astype(jnp.bfloat16), preferred_element_type=jnp.float32)
    slots = jnp.sum(jnp.where(onehot, running, 0.0), axis=1).astype(jnp.int32) - 1
    place = assign * capacity + slots
    pack = (place[None, :] == jnp.arange(experts * capacity, dtype=jnp.int32)[:, None]).astype(
        jnp.bfloat16
    )
    packed = jnp.dot(pack, tokens, preferred_element_type=jnp.float32).astype(jnp.bfloat16)
    mine = lax.all_to_all(
        packed.reshape(experts, capacity, width), "expert", split_axis=0, concat_axis=0, tiled=True
    )
    rows = lax.all_gather(mine.reshape(experts * capacity, width), "dp", axis=0, tiled=True)
    raw = jnp.dot(rows, first, preferred_element_type=jnp.float32)
    hidden = jax.nn.gelu(raw, approximate=True).astype(jnp.bfloat16)
    partial = jnp.dot(hidden, second, preferred_element_type=jnp.float32).astype(jnp.bfloat16)
    summed = lax.psum_scatter(partial, "dp", scatter_dimension=0, tiled=True)
    returned = lax.all_to_all(
        summed.reshape(experts, capacity, width), "expert", split_axis=0, concat_axis=0, tiled=True
    ).reshape(experts * capacity, width)
    picked = lax.dot_general(
        pack, returned, (((0,), (0,)), ((), ())), preferred_element_type=jnp.float32
    )
    gate = jax.nn.sigmoid(own)
    mixed = (gate[:, None] * picked).astype(jnp.bfloat16)
    return (mixed, new_price)


def solution(mesh):
    return jax.shard_map(
        shards,
        mesh=mesh,
        in_specs=(
            P(("dp", "expert"), None),
            P(),
            P(),
            P("expert", None, "dp"),
            P("expert", "dp", None),
            P(("dp", "expert")),
        ),
        out_specs=(P(("dp", "expert"), None), P()),
        check_vma=False,
    )
```

profile of v0, /device:TPU:0, one launch (start us, length us, event | category | flops | bytes accessed | tf_op | source)
XLA Modules:
  0.0 268.7 jit_solution(14354729918108742788)
XLA Ops:
  7.2 0.0 copy-start
  7.2 0.0 all-gather.2.cloned.1.call-start
  7.2 0.9 fusion.21
  8.1 0.7 add_add_fusion
  8.8 0.0 copy-done
  8.8 0.0 copy-start.2
  8.8 0.6 convolution_convert_fusion
  9.4 44.2 %all_to_all.10 = bf16[8,24,4096]{2,1,0:T(8,128)(2,1)} all-to-all(bf16[8,24,4096]{2,1,0:T(8,128)(2,1)S(1)} %bitcast.23), channel_id=1, replica_groups=mesh['dp'=4,'expert'=8] {'expert'}, dimensions={0} | all-to-all | bytes 3145728 | tf_op jit(solution)/shard_map/all_to_all | solution.py:33
  53.6 0.0 copy-done.2
  53.6 0.0 all-gather.2.cloned.1.call-update
  53.6 0.0 reduce-scatter.2.cloned.1.call-start
  53.6 45.5 %all-gather.2.cloned.1.call-done = bf16[768,4096]{1,0:T(8,128)(2,1)} async-done(((bf16[192,4096]{1,0:T(8,128)(2,1)}), bf16[768,4096]{1,0:T(8,128)(2,1)}) %all-gather.2.cloned.1.call-update) | async-done | bytes 6291472 | tf_op jit(solution)/shard_map/all_gather | solution.py:36
  99.1 40.2 %fusion.4 = bf16[768,4096]{1,0:T(8,128)(2,1)} fusion(bf16[1,2048,4096]{2,1,0:T(8,128)(2,1)} %param.10, bf16[768,4096]{1,0:T(8,128)(2,1)} %all-gather.2.cloned.1.call-done, bf16[1,4096,2048]{2,1,0:T(8,128)(2,1)} %param.9), kind=kOutput, calls=%fused_computation.5 | convolution fusion | flops 25787105280 | bytes 46137344 | tf_op jit(solution)/shard_map/dot_general | solution.py:39
  139.4 0.0 copy-start.1
  139.4 0.0 copy-start.4
  139.4 0.0 copy-start.5
  139.4 0.0 copy-start.3
  139.4 0.0 reduce-scatter.2.cloned.1.call-update
  139.4 58.5 %reduce-scatter.2.cloned.1.call-done = bf16[192,4096]{1,0:T(8,128)(2,1)} async-done(((bf16[768,4096]{1,0:T(8,128)(2,1)}), bf16[192,4096]{1,0:T(8,128)(2,1)}) %reduce-scatter.2.cloned.1.call-update) | async-done | bytes 1572880 | tf_op jit(solution)/shard_map/reduce_scatter | solution.py:40
  197.9 5.5 %all-to-all-start.1 = ((bf16[8,24,4096]{2,1,0:T(8,128)(2,1)}), bf16[8,24,4096]{2,1,0:T(8,128)(2,1)S(1)}, u32[]{:S(2)}, u32[]{:S(2)}) async-start(bf16[8,24,4096]{2,1,0:T(8,128)(2,1)} %bitcast.24), calls=%async_computation.2 | async-start | bytes 3145728 | tf_op jit(solution)/shard_map/all_to_all | solution.py:41
  203.5 0.0 copy-done.1
  203.5 0.0 copy-done.4
  203.5 0.0 copy-done.5
  203.5 0.4 select_reduce_fusion.1
  203.9 0.1 select_reduce_fusion
  204.0 56.3 %pmax.7 = f32[8]{0:T(128)} all-reduce(f32[8]{0:T(128)S(1)} %select_reduce_fusion), channel_id=1, replica_groups=mesh['dp'=4,'expert'=8] {'dp','expert'}, use_global_device_ids=true, to_apply=%region_5.6 | all-reduce | flops 8 | bytes 64 | tf_op jit(solution)/shard_map/pmax | solution.py:22
  260.3 0.0 all-to-all-done.1
  260.3 0.0 copy-done.3
  260.3 1.5 fusion.15
  (1 shorter events, 0.0 us)
Async XLA Ops:
  7.2 1.6 copy-start
  7.2 92.0 %all-gather.2.cloned.1.call-start = ((), (), s32[]{:S(2)}) async-start(), calls=%async_computation.3 | async-start | bytes 7864320 | tf_op jit(solution)/shard_map/all_gather | solution.py:36
  8.8 44.8 %copy-start.2 = (s32[128]{0:T(128)}, s32[128]{0:T(128)S(1)}, u32[]{:S(2)}) copy-start(s32[128]{0:T(128)S(1)} %add_add_fusion) | copy-start | bytes 1540
  53.6 144.3 %reduce-scatter.2.cloned.1.call-start = ((), (), s32[]{:S(2)}) async-start(), calls=%async_computation.4 | async-start | bytes 7864320 | tf_op jit(solution)/shard_map/reduce_scatter | solution.py:40
  139.4 64.1 %copy-start.1 = (bf16[4096,8]{0,1:T(8,128)(2,1)S(1)}, bf16[4096,8]{0,1:T(8,128)(2,1)}, u32[]{:S(2)}) copy-start(bf16[4096,8]{0,1:T(8,128)(2,1)} %param.7) | copy-start | bytes 196612
  139.4 64.1 %copy-start.4 = (f32[8]{0:T(128)S(1)}, f32[8]{0:T(128)}, u32[]{:S(2)}) copy-start(f32[8]{0:T(128)} %param.8) | copy-start | bytes 100
  139.4 64.1 %copy-start.5 = (s32[128]{0:T(128)S(1)}, s32[128]{0:T(128)}, u32[]{:S(2)}) copy-start(s32[128]{0:T(128)} %param.11) | copy-start | bytes 1540
  139.4 121.0 %copy-start.3 = (s32[128]{0:T(128)S(1)}, s32[128]{0:T(128)}, u32[]{:S(2)}) copy-start(s32[128]{0:T(128)} %copy-done.2) | copy-start | bytes 1540
  197.9 62.4 %all-to-all-start.1 = ((bf16[8,24,4096]{2,1,0:T(8,128)(2,1)}), bf16[8,24,4096]{2,1,0:T(8,128)(2,1)S(1)}, u32[]{:S(2)}, u32[]{:S(2)}) async-start(bf16[8,24,4096]{2,1,0:T(8,128)(2,1)} %bitcast.24), calls=%async_computation.2 | async-start | bytes 3145728 | tf_op jit(solution)/shard_map/all_to_all | solution.py:41
Sparse Core Ops, SparseCore 0:
  53.7 45.3 all-gather.1
  139.5 58.3 reduce-scatter.1
where the time goes:
time: 269 us
  waiting for transfers between devices  104 us (39%)
  blocking collectives  101 us (38%)
  matrix products  43.6 us (16%)
  between operations  14.1 us (5%)
  starting transfers between devices  5.59 us (2%)
    reduce_scatter x1, waiting for transfers between devices, shards(): summed = lax.psum_scatter(partial, 'dp', scatter_dimension=0, tiled=True)  58.5 us
    pmax x1, blocking collectives, shards(): new_price = lax.pmax(local_best, ('dp', 'expert'))  56.3 us
    all_gather x1, waiting for transfers between devices, shards(): lax.all_gather(mine.reshape(experts * capacity, width), 'dp', axis=0, til...  45.5 us
    all_to_all x1, blocking collectives, shards(): lax.all_to_all(packed.reshape(experts, capacity, width), 'expert', split_...  44.2 us
    dot_general x1, matrix products, shards(): jnp.dot(hidden, second, preferred_element_type=jnp.float32)  40.2 us
    all_to_all x1, starting transfers between devices, shards(): lax.all_to_all(summed.reshape(experts, capacity, width), 'expert', split_...  5.51 us
  transfers between devices with their start and end apart: 3, of which 2 were waited for; matrix products, arithmetic and copies ran while one was open for 0% of the time, Pallas kernels for 0%

commit v1 on v0

--- a/solution.py
+++ b/solution.py
@@ -2,8 +2,41 @@
 import jax.numpy as jnp
 from jax import lax
 from jax.sharding import PartitionSpec as P
+from jax.lax import axis_index, axis_size, ppermute
 
 BID_STEP = 0.01
+
+
+def group_yards(message, dim_k, x0):
+    part_next = message.shape
+    value_now = message.reshape(
+        *part_next[:dim_k], x0, part_next[dim_k] // x0, *part_next[dim_k + 1 :]
+    )
+    q_next = jnp.moveaxis(value_now, dim_k, 0)
+    return q_next
+
+
+def update_seats_all(load, out_dim):
+    load = jnp.moveaxis(load, 0, out_dim)
+    after = load.shape
+    a_next = load.reshape(
+        *after[:out_dim], after[out_dim] * after[out_dim + 1], *after[out_dim + 2 :]
+    )
+    return a_next
+
+
+def _make_heads(z, net_axis, here_x, u_in):
+    e_now, reply = (axis_size(net_axis), axis_index(net_axis))
+    finding = group_yards(z, here_x, e_now)
+    blocks_here = [finding[reply]]
+    for hop_no in [*range(1, e_now)]:
+        val2 = finding[(reply + hop_no) % e_now]
+        blocks_here.append(
+            ppermute(val2, net_axis, [(ii, (ii + hop_no) % e_now) for ii in range(e_now)])
+        )
+    finding = jnp.stack(blocks_here)[(reply - jnp.arange(e_now)) % e_now]
+    passed = update_seats_all(finding, u_in)
+    return passed
 
 
 def shards(tokens, router, price, w_in, w_out, assign):
@@ -38,9 +71,9 @@
     hidden = jax.nn.gelu(raw, approximate=True).astype(jnp.bfloat16)
     partial = jnp.dot(hidden, second, preferred_element_type=jnp.float32).astype(jnp.bfloat16)
     summed = lax.psum_scatter(partial, "dp", scatter_dimension=0, tiled=True)
-    returned = lax.all_to_all(
-        summed.reshape(experts, capacity, width), "expert", split_axis=0, concat_axis=0, tiled=True
-    ).reshape(experts * capacity, width)
+    returned = _make_heads(summed.reshape(experts, capacity, width), "expert", 0, 0).reshape(
+        experts * capacity, width
+    )
     picked = lax.dot_general(
         pack, returned, (((0,), (0,)), ((), ())), preferred_element_type=jnp.float32
     )

time: 269 us -> 249 us (0.926)
  the two profiles are of different devices: /device:TPU:0 before, /device:TPU:13 now
where the time goes in v1:
time: 249 us
  waiting for transfers between devices  98.4 us (40%)
  blocking collectives  78.8 us (32%)
  matrix products  43.6 us (18%)
  between operations  14.2 us (6%)
  starting transfers between devices  7.25 us (3%)
  local copies, waits for them, and re-layouts  5.73 us (2%)
    all_gather x1, waiting for transfers between devices, shards(): lax.all_gather(mine.reshape(experts * capacity, width), 'dp', axis=0, til...  49.1 us
    dot_general x1, matrix products, shards(): jnp.dot(hidden, second, preferred_element_type=jnp.float32)  40.3 us
    all_to_all x1, blocking collectives, shards(): lax.all_to_all(packed.reshape(experts, capacity, width), 'expert', split_...  39.4 us
    pmax x1, blocking collectives, shards(): new_price = lax.pmax(local_best, ('dp', 'expert'))  39.4 us
    ppermute x7, waiting for transfers between devices, _make_heads(): ppermute(val2, net_axis, [(ii, (ii + hop_no) % e_now) for ii in range(e_n...  31.2 us
    reduce_scatter x1, waiting for transfers between devices, shards(): summed = lax.psum_scatter(partial, 'dp', scatter_dimension=0, tiled=True)  18 us
    ppermute x7, starting transfers between devices, _make_heads(): ppermute(val2, net_axis, [(ii, (ii + hop_no) % e_now) for ii in range(e_n...  7.17 us
  transfers between devices with their start and end apart: 9, of which 7 were waited for; matrix products, arithmetic and copies ran while one was open for 0% of the time, Pallas kernels for 0%

profile of v1, /device:TPU:13, one launch (start us, length us, event | category | flops | bytes accessed | tf_op | source)
XLA Modules:
  0.0 248.8 jit_solution(2362474822837224471)
XLA Ops:
  7.2 0.0 copy-start
  7.2 0.0 all-gather.2.cloned.1.call-start
  7.2 0.9 fusion.21
  8.1 0.7 add_add_fusion
  8.8 0.6 convolution_convert_fusion
  9.4 39.4 %all_to_all.5 = bf16[8,24,4096]{2,1,0:T(8,128)(2,1)} all-to-all(bf16[8,24,4096]{2,1,0:T(8,128)(2,1)S(1)} %bitcast.53), channel_id=1, replica_groups=mesh['dp'=4,'expert'=8] {'expert'}, dimensions={0} | all-to-all | bytes 3145728 | tf_op jit(solution)/shard_map/all_to_all | solution.py:66
  48.8 0.0 all-gather.2.cloned.1.call-update
  48.8 0.0 reduce-scatter.2.cloned.1.call-start
  48.9 49.1 %all-gather.2.cloned.1.call-done = bf16[768,4096]{1,0:T(8,128)(2,1)} async-done(((bf16[192,4096]{1,0:T(8,128)(2,1)}), bf16[768,4096]{1,0:T(8,128)(2,1)}) %all-gather.2.cloned.1.call-update) | async-done | bytes 6291472 | tf_op jit(solution)/shard_map/all_gather | solution.py:69
  98.0 40.3 %fusion.4 = bf16[768,4096]{1,0:T(8,128)(2,1)} fusion(bf16[1,2048,4096]{2,1,0:T(8,128)(2,1)} %param.10, bf16[768,4096]{1,0:T(8,128)(2,1)} %all-gather.2.cloned.1.call-done, bf16[1,4096,2048]{2,1,0:T(8,128)(2,1)} %param.9), kind=kOutput, calls=%fused_computation.6 | convolution fusion | flops 25787105280 | bytes 46137344 | tf_op jit(solution)/shard_map/dot_general | solution.py:72
  138.2 0.0 reduce-scatter.2.cloned.1.call-update
  138.3 0.8 copy-done.2
  139.1 0.4 select_reduce_fusion.1
  139.5 0.1 select_reduce_fusion
  139.6 39.4 %pmax.7 = f32[8]{0:T(128)} all-reduce(f32[8]{0:T(128)S(1)} %select_reduce_fusion), channel_id=1, replica_groups=mesh['dp'=4,'expert'=8] {'dp','expert'}, use_global_device_ids=true, to_apply=%region_5.6 | all-reduce | flops 8 | bytes 64 | tf_op jit(solution)/shard_map/pmax | solution.py:55
  179.0 18.0 %reduce-scatter.2.cloned.1.call-done = bf16[192,4096]{1,0:T(8,128)(2,1)} async-done(((bf16[768,4096]{1,0:T(8,128)(2,1)}), bf16[192,4096]{1,0:T(8,128)(2,1)}) %reduce-scatter.2.cloned.1.call-update) | async-done | bytes 1572880 | tf_op jit(solution)/shard_map/reduce_scatter | solution.py:73
  197.1 1.6 dynamic-slice_bitcast_fusion
  198.7 1.2 collective-permute-start
  199.9 1.3 collective-permute-start.1
  201.2 1.1 collective-permute-start.2
  202.3 1.2 collective-permute-start.3
  203.6 1.1 collective-permute-start.4
  204.7 1.2 collective-permute-start.5
  205.9 2.8 %collective-permute-done.1 = bf16[1,24,4096]{2,1,0:T(8,128)(2,1)S(1)} collective-permute-done((bf16[1,24,4096]{2,1,0:T(8,128)(2,1)S(1)}, bf16[1,24,4096]{2,1,0:T(8,128)(2,1)S(1)}, u32[]{:S(2)}, u32[]{:S(2)}) %collective-permute-start.1) | collective-permute-done | bytes 196640 | tf_op jit(solution)/shard_map/ppermute | solution.py:35
  208.7 20.1 %collective-permute-done.2 = bf16[1,24,4096]{2,1,0:T(8,128)(2,1)S(1)} collective-permute-done((bf16[1,24,4096]{2,1,0:T(8,128)(2,1)S(1)}, bf16[1,24,4096]{2,1,0:T(8,128)(2,1)S(1)}, u32[]{:S(2)}, u32[]{:S(2)}) %collective-permute-start.2) | collective-permute-done | bytes 196640 | tf_op jit(solution)/shard_map/ppermute | solution.py:35
  228.8 4.2 %collective-permute-done.3 = bf16[1,24,4096]{2,1,0:T(8,128)(2,1)S(1)} collective-permute-done((bf16[1,24,4096]{2,1,0:T(8,128)(2,1)S(1)}, bf16[1,24,4096]{2,1,0:T(8,128)(2,1)S(1)}, u32[]{:S(2)}, u32[]{:S(2)}) %collective-permute-start.3) | collective-permute-done | bytes 196640 | tf_op jit(solution)/shard_map/ppermute | solution.py:35
  233.0 0.0 copy-start.4
  233.0 2.9 %collective-permute-done.5 = bf16[1,24,4096]{2,1,0:T(8,128)(2,1)S(1)} collective-permute-done((bf16[1,24,4096]{2,1,0:T(8,128)(2,1)S(1)}, bf16[1,24,4096]{2,1,0:T(8,128)(2,1)S(1)}, u32[]{:S(2)}, u32[]{:S(2)}) %collective-permute-start.5) | collective-permute-done | bytes 196640 | tf_op jit(solution)/shard_map/ppermute | solution.py:35
  236.0 1.2 collective-permute-done.6
  237.2 1.1 copy-done.1
  238.4 2.1 gather_fusion
  240.5 1.5 fusion.15
  (23 shorter events, 0.2 us)
Async XLA Ops:
  7.2 1.6 copy-start
  7.2 90.8 %all-gather.2.cloned.1.call-start = ((), (), s32[]{:S(2)}) async-start(), calls=%async_computation.2 | async-start | bytes 7864320 | tf_op jit(solution)/shard_map/all_gather | solution.py:69
  8.8 40.0 %copy-start.3 = (s32[128]{0:T(128)}, s32[128]{0:T(128)S(1)}, u32[]{:S(2)}) copy-start(s32[128]{0:T(128)S(1)} %add_add_fusion) | copy-start | bytes 1540
  48.8 148.2 %reduce-scatter.2.cloned.1.call-start = ((), (), s32[]{:S(2)}) async-start(), calls=%async_computation.3 | async-start | bytes 7864320 | tf_op jit(solution)/shard_map/reduce_scatter | solution.py:73
  138.2 0.8 copy-start.2
  138.2 0.8 copy-start.5
  138.2 0.8 copy-start.6
  198.7 6.0 %collective-permute-start = (bf16[1,24,4096]{2,1,0:T(8,128)(2,1)S(1)}, bf16[1,24,4096]{2,1,0:T(8,128)(2,1)S(1)}, u32[]{:S(2)}, u32[]{:S(2)}) collective-permute-start(bf16[1,24,4096]{2,1,0:T(8,128)(2,1)S(1)} %get-tuple-element.10), channel_id=1, source_target_pairs={{0,1},{1,2},{2,3},{3,4},{4,5},{5,6},{6,7},{7,0},{8,9},{9,10},{10,1... | collective-permute-start | bytes 589832 | tf_op jit(solution)/shard_map/ppermute | solution.py:35
  199.9 8.8 %collective-permute-start.1 = (bf16[1,24,4096]{2,1,0:T(8,128)(2,1)S(1)}, bf16[1,24,4096]{2,1,0:T(8,128)(2,1)S(1)}, u32[]{:S(2)}, u32[]{:S(2)}) collective-permute-start(bf16[1,24,4096]{2,1,0:T(8,128)(2,1)S(1)} %get-tuple-element.9), channel_id=1, source_target_pairs={{0,2},{1,3},{2,4},{3,5},{4,6},{5,7},{6,0},{7,1},{8,10},{9,11},{10,... | collective-permute-start | bytes 589832 | tf_op jit(solution)/shard_map/ppermute | solution.py:35
  201.2 27.6 %collective-permute-start.2 = (bf16[1,24,4096]{2,1,0:T(8,128)(2,1)S(1)}, bf16[1,24,4096]{2,1,0:T(8,128)(2,1)S(1)}, u32[]{:S(2)}, u32[]{:S(2)}) collective-permute-start(bf16[1,24,4096]{2,1,0:T(8,128)(2,1)S(1)} %get-tuple-element.8), channel_id=1, source_target_pairs={{0,3},{1,4},{2,5},{3,6},{4,7},{5,0},{6,1},{7,2},{8,11},{9,12},{10,... | collective-permute-start | bytes 589832 | tf_op jit(solution)/shard_map/ppermute | solution.py:35
  202.3 30.7 %collective-permute-start.3 = (bf16[1,24,4096]{2,1,0:T(8,128)(2,1)S(1)}, bf16[1,24,4096]{2,1,0:T(8,128)(2,1)S(1)}, u32[]{:S(2)}, u32[]{:S(2)}) collective-permute-start(bf16[1,24,4096]{2,1,0:T(8,128)(2,1)S(1)} %get-tuple-element.7), channel_id=1, source_target_pairs={{0,4},{1,5},{2,6},{3,7},{4,0},{5,1},{6,2},{7,3},{8,12},{9,13},{10,... | collective-permute-start | bytes 589832 | tf_op jit(solution)/shard_map/ppermute | solution.py:35
  203.6 29.5 %collective-permute-start.4 = (bf16[1,24,4096]{2,1,0:T(8,128)(2,1)S(1)}, bf16[1,24,4096]{2,1,0:T(8,128)(2,1)S(1)}, u32[]{:S(2)}, u32[]{:S(2)}) collective-permute-start(bf16[1,24,4096]{2,1,0:T(8,128)(2,1)S(1)} %get-tuple-element.6), channel_id=1, source_target_pairs={{0,5},{1,6},{2,7},{3,0},{4,1},{5,2},{6,3},{7,4},{8,13},{9,14},{10,... | collective-permute-start | bytes 589832 | tf_op jit(solution)/shard_map/ppermute | solution.py:35
  204.7 31.3 %collective-permute-start.5 = (bf16[1,24,4096]{2,1,0:T(8,128)(2,1)S(1)}, bf16[1,24,4096]{2,1,0:T(8,128)(2,1)S(1)}, u32[]{:S(2)}, u32[]{:S(2)}) collective-permute-start(bf16[1,24,4096]{2,1,0:T(8,128)(2,1)S(1)} %get-tuple-element.5), channel_id=1, source_target_pairs={{0,6},{1,7},{2,0},{3,1},{4,2},{5,3},{6,4},{7,5},{8,14},{9,15},{10,... | collective-permute-start | bytes 589832 | tf_op jit(solution)/shard_map/ppermute | solution.py:35
  208.7 28.5 %collective-permute-start.6 = (bf16[1,24,4096]{2,1,0:T(8,128)(2,1)S(1)}, bf16[1,24,4096]{2,1,0:T(8,128)(2,1)S(1)}, u32[]{:S(2)}, u32[]{:S(2)}) collective-permute-start(bf16[1,24,4096]{2,1,0:T(8,128)(2,1)S(1)} %get-tuple-element.4), channel_id=1, source_target_pairs={{0,7},{1,0},{2,1},{3,2},{4,3},{5,4},{6,5},{7,6},{8,15},{9,8},{10,9... | collective-permute-start | bytes 589832 | tf_op jit(solution)/shard_map/ppermute | solution.py:35
  233.0 7.4 %copy-start.4 = (s32[128]{0:T(128)S(1)}, s32[128]{0:T(128)}, u32[]{:S(2)}) copy-start(s32[128]{0:T(128)} %copy-done.3) | copy-start | bytes 1540
  237.2 1.2 copy-start.1
Sparse Core Ops, SparseCore 0:
  48.9 48.9 all-gather.1
  138.4 58.6 reduce-scatter.1
